TPU v7x, 512 devices: a whole 4x4x16 slice. The times are simulated.
512 devices in a mesh: head: 8 (over y, core), frame: 64 (over x, z).
Axes of the slice: x: 4, y: 4, z: 16, core: 2. Of those that a mesh axis runs over, the one named last changes fastest.
Arguments:
- queries: bfloat16 [65536, 16, 128], P(('frame', 'head')), may hold values from -30 to 30
- keys: bfloat16 [65536, 16, 128], P(('frame', 'head')), may hold values from -4 to 4
- values: bfloat16 [65536, 16, 128], P(('frame', 'head')), may hold values from -24 to 24
- block_mask: int32 [64, 16, 16], replicated, may hold values from 0 to 1, as said below
- strides: int32 [64], replicated, may hold values from 1 to 16, as said below
- offsets: int32 [64], replicated, may hold values from 0 to 15
Outputs:
- attended: bfloat16 [65536, 16, 128], P(('frame', 'head'))
Inputs may be any that keep to these rules, and one draw needn't show every extreme that they name: Every diagonal entry block_mask[i, b, b] is 1. strides[0] is 1, strides[1] is 4, 8 or 16, and every later entry is 8 or 16.
All inputs are finite; a program needn't handle non-finite values.
Results may differ from a plain program's by a relative error of at most 0.0043.
Values may be sent and summed in bfloat16 or wider, within the bound.
No kernel may reach another device: no remote copies, remote signals or barrier semaphores. Data moves between devices by JAX's collectives and lax.ppermute only.
A program may use at most 64 MiB of HBM per device.

v0:
```python
import jax
import jax.numpy as jnp
from jax import lax
from jax.sharding import PartitionSpec as P

masked_score = -1e30


def passed_along(block, axis, distance):
    devices = range(lax.axis_size(axis))
    route = [(i - distance, i) for i in devices if i - distance in devices]
    return lax.ppermute(block, axis, route)


def group_terms(query_blocks, key_rows, value_rows, keep_mask, score_scale):
    scores = (
        jnp.einsum("qahd,gnhd->hqagn", query_blocks, key_rows, preferred_element_type=jnp.float32)
        * score_scale
    )
    allowed = keep_mask[None, :, None, :, :]
    scores = jnp.where(allowed, scores, masked_score)
    group_tops = jnp.max(scores, axis=4)
    weights = jnp.where(allowed, jnp.exp(scores - group_tops[..., None]), 0.0)
    group_totals = jnp.sum(weights, axis=4)
    group_sums = jnp.einsum(
        "hqagn,gnhd->hqagd",
        weights.astype(jnp.bfloat16),
        value_rows,
        preferred_element_type=jnp.float32,
    )
    return (group_tops, group_totals, group_sums)


def absorb(carry_state, group_tops, group_totals, group_sums):
    running_top, running_total, running_sum = carry_state
    new_top = jnp.maximum(running_top, jnp.max(group_tops, axis=3))
    shrink = jnp.exp(running_top - new_top)
    factors = jnp.exp(group_tops - new_top[..., None])
    running_total = running_total * shrink + jnp.sum(factors * group_totals, axis=3)
    running_sum = running_sum * shrink[..., None] + jnp.sum(factors[..., None] * group_sums, axis=3)
    return (new_top, running_total, running_sum)


def pick_blocks(key_blocks, value_blocks, offsets, source_frame, spacing, block_count):
    first_block = (spacing - offsets[source_frame] % spacing) % spacing
    chosen = first_block + spacing * jnp.arange(block_count, dtype=jnp.int32)
    return jnp.stack([jnp.take(key_blocks, chosen, axis=0), jnp.take(value_blocks, chosen, axis=0)])


def local(queries, keys, values, block_mask, strides, offsets):
    local_queries, local_keys, local_values = (
        lax.all_to_all(queries, "head", split_axis=1, concat_axis=0, tiled=True),
        lax.all_to_all(keys, "head", split_axis=1, concat_axis=0, tiled=True),
        lax.all_to_all(values, "head", split_axis=1, concat_axis=0, tiled=True),
    )
    frame_rows, heads_here, head_dim = local_queries.shape
    frame_blocks = block_mask.shape[1]
    block_rows = frame_rows // frame_blocks
    score_scale = head_dim ** (-0.5)
    frame_index = lax.axis_index("frame")
    frame_total = lax.axis_size("frame")
    query_blocks = local_queries.reshape(frame_blocks, block_rows, heads_here, head_dim)
    key_blocks = local_keys.reshape(frame_blocks, block_rows, heads_here, head_dim)
    value_blocks = local_values.reshape(frame_blocks, block_rows, heads_here, head_dim)
    own_mask = lax.dynamic_index_in_dim(block_mask, frame_index, 0, keepdims=False) == 1
    carry_state = (
        jnp.full((heads_here, frame_blocks, block_rows), masked_score, jnp.float32),
        jnp.zeros((heads_here, frame_blocks, block_rows), jnp.float32),
        jnp.zeros((heads_here, frame_blocks, block_rows, head_dim), jnp.float32),
    )
    half_blocks = frame_blocks // 2
    whole_keys = local_keys.reshape(1, frame_rows, heads_here, head_dim)
    whole_values = local_values.reshape(1, frame_rows, heads_here, head_dim)
    results = []
    for first_block in (0, half_blocks):
        keep_mask = jnp.repeat(
            own_mask[first_block : first_block + half_blocks], block_rows, axis=1
        )[:, None, :]
        results.append(
            group_terms(
                query_blocks[first_block : first_block + half_blocks],
                whole_keys,
                whole_values,
                keep_mask,
                score_scale,
            )
        )
    carry_state = absorb(
        carry_state,
        jnp.concatenate([entry[0] for entry in results], axis=1),
        jnp.concatenate([entry[1] for entry in results], axis=1),
        jnp.concatenate([entry[2] for entry in results], axis=1),
    )
    for distance in (1, 2, 3):
        spacing = frame_blocks // 4 if distance == 1 else frame_blocks // 2
        block_count = frame_blocks // spacing
        packed = pick_blocks(key_blocks, value_blocks, offsets, frame_index, spacing, block_count)
        for direction in (1, -1):
            arrived = passed_along(packed, "frame", direction * distance)
            source_frame = frame_index - direction * distance
            valid = (source_frame >= 0) & (source_frame < frame_total)
            clipped = jnp.clip(source_frame, 0, frame_total - 1)
            chosen = (spacing - offsets[clipped] % spacing) % spacing + spacing * jnp.arange(
                block_count, dtype=jnp.int32
            )
            attend_phase_ok = (chosen + offsets[clipped]) % strides[distance] == 0
            attend_kept = valid & own_mask[:, chosen] & attend_phase_ok[None, :]
            attend_keep_mask = jnp.repeat(attend_kept, block_rows, axis=1)[:, None, :]
            near_keys = arrived[0].reshape(1, block_count * block_rows, heads_here, head_dim)
            near_values = arrived[1].reshape(1, block_count * block_rows, heads_here, head_dim)
            carry_state = absorb(
                carry_state,
                *group_terms(query_blocks, near_keys, near_values, attend_keep_mask, score_scale)
            )
    anchor_block = (frame_blocks - offsets[frame_index] % frame_blocks) % frame_blocks
    anchor_pair = jnp.stack([key_blocks[anchor_block], value_blocks[anchor_block]])[None]
    gathered = lax.all_gather(anchor_pair, "frame", axis=0, tiled=True)
    piece_frames = gathered.shape[0]
    group_width = 4
    grouped = gathered.reshape(
        piece_frames // group_width, group_width, 2, block_rows, heads_here, head_dim
    )

    def one_group(state_inner, entry):
        group_blocks, group_number = entry
        sources = 0 + group_number * group_width + jnp.arange(group_width, dtype=jnp.int32)
        distances = jnp.abs(frame_index - sources)
        spots = (frame_blocks - offsets[sources] % frame_blocks) % frame_blocks
        phase_ok = (spots + offsets[sources]) % strides[distances] == 0
        kept = (distances >= 4)[None, :] & own_mask[:, spots] & phase_ok[None, :]
        keep_mask = jnp.repeat(kept, block_rows, axis=1).reshape(
            frame_blocks, group_width, block_rows
        )
        terms = group_terms(
            query_blocks, group_blocks[:, 0], group_blocks[:, 1], keep_mask, score_scale
        )
        return (absorb(state_inner, *terms), None)

    numbers = jnp.arange(piece_frames // group_width, dtype=jnp.int32)
    state_out, unused = lax.scan(one_group, carry_state, (grouped, numbers))
    carry_state = state_out
    running_top, running_total, running_sum = carry_state
    output = (running_sum / running_total[..., None]).astype(jnp.bfloat16)
    output = jnp.transpose(output, (1, 2, 0, 3)).reshape(frame_rows, heads_here, head_dim)
    return lax.all_to_all(output, "head", split_axis=0, concat_axis=1, tiled=True)


def solution(mesh):
    placed = (
        P(("frame", "head"), None, None),
        P(("frame", "head"), None, None),
        P(("frame", "head"), None, None),
        P(),
        P(),
        P(),
    )
    return jax.shard_map(
        local,
        mesh=mesh,
        in_specs=placed,
        out_specs=P(("frame", "head"), None, None),
        check_vma=False,
    )
```

profile of v0, /device:TPU:1, one launch (start us, length us, event | category | flops | bytes accessed | tf_op | source)
XLA Modules:
  0.0 511.0 jit_solution(10326645621186077479)
XLA Ops:
  8.6 10.2 %all-to-all-start.1 = ((bf16[128,16,128]{2,0,1:T(8,128)(2,1)}), bf16[128,16,128]{2,0,1:T(8,128)(2,1)S(1)}, u32[]{:S(2)}, u32[]{:S(2)}) async-start(bf16[128,16,128]{2,0,1:T(8,128)(2,1)} %copy.119), calls=%async_computation.1 | async-start | bytes 1048576 | tf_op jit(solution)/shard_map/all_to_all | solution.py:53
  49.3 4.8 all-to-all-start.2
  63.5 4.4 all-to-all-start
  71.7 4.0 collective-permute-start
  79.0 7.0 %collective-permute-start.4 = (bf16[2,2,64,2,128]{4,2,3,1,0:T(8,128)(2,1)S(1)}, bf16[2,2,64,2,128]{4,2,3,1,0:T(8,128)(2,1)S(1)}, u32[]{:S(2)}, u32[]{:S(2)}) collective-permute-start(bf16[2,2,64,2,128]{4,2,3,1,0:T(8,128)(2,1)S(1)} %pad_maximum_fusion.1), channel_id=1, source_target_pairs={{0,3},{1,4},{2,5},{3,6},{4,7},{5,8},{6,9},{7,10},{8,11},{9,12},{10... | collective-permute-start | bytes 393224 | tf_op jit(solution)/shard_map/ppermute | solution.py:12
  90.2 2.7 fusion.21
  97.3 7.7 %collective-permute-done.3 = bf16[2,2,64,2,128]{4,2,3,1,0:T(8,128)(2,1)S(1)} collective-permute-done((bf16[2,2,64,2,128]{4,2,3,1,0:T(8,128)(2,1)S(1)}, bf16[2,2,64,2,128]{4,2,3,1,0:T(8,128)(2,1)S(1)}, u32[]{:S(2)}, u32[]{:S(2)}) %collective-permute-start.3) | collective-permute-done | bytes 131104 | tf_op jit(solution)/shard_map/ppermute | solution.py:12
  120.8 3.0 fusion.58
  123.7 103.3 %all-gather.3.cloned.1.call-done = bf16[128,64,2,128]{3,1,0,2:T(8,128)(2,1)} async-done(((bf16[2,64,2,128]{3,1,0,2:T(8,128)(2,1)}), bf16[128,64,2,128]{3,1,0,2:T(8,128)(2,1)}) %all-gather.3.cloned.1.call-update) | async-done | bytes 4194320 | tf_op jit(solution)/shard_map/all_gather | solution.py:117
  227.0 250.4 %while.16 = (s32[]{:T(128)}, f32[2,16,64]{2,1,0:T(8,128)S(1)}, f32[2,16,64]{2,1,0:T(8,128)S(1)}, f32[2,16,64,128]{3,2,1,0:T(8,128)}, s32[]{:T(128)}, /*index=5*/...) while((s32[]{:T(128)}, f32[2,16,64]{2,1,0:T(8,128)S(1)}, ...), condition=%wide.region_22.25_spmd, body=%wide.region_16.24_spmd.sunk | while | flops 276053440 | bytes 31036728 | solution.py:140
  234.9 2.7 copy.175
  250.5 2.7 copy.175
  266.2 2.7 copy.175
  281.8 2.7 copy.175
  297.5 2.7 copy.175
  313.1 2.7 copy.175
  328.8 2.7 copy.175
  360.1 2.7 copy.175
  375.7 2.7 copy.175
  391.4 2.7 copy.175
  438.3 2.7 copy.175
  453.9 2.7 copy.175
  469.6 2.7 copy.175
  479.5 23.4 %all_to_all.63 = bf16[1024,2,128]{2,1,0:T(2,128)(2,1)S(1)} all-to-all(bf16[1024,2,128]{2,1,0:T(2,128)(2,1)S(1)} %bitcast.475), channel_id=1, replica_groups=mesh['head'=8,'frame'=64] {'head'}, dimensions={0} | all-to-all | bytes 1048576 | tf_op jit(solution)/shard_map/all_to_all | solution.py:145
  (588 shorter events, 262.5 us)
Async XLA Ops:
  6.5 33.9 %copy-start = (s32[64,16,16]{0,2,1:T(8,128)S(1)}, s32[64,16,16]{0,2,1:T(8,128)}, u32[]{:S(2)}) copy-start(s32[64,16,16]{0,2,1:T(8,128)} %param.15) | copy-start | bytes 196612
  6.5 47.7 %copy-start.5 = (bf16[128,16,128]{2,1,0:T(8,128)(2,1)S(1)}, bf16[128,16,128]{2,1,0:T(8,128)(2,1)}, u32[]{:S(2)}) copy-start(bf16[128,16,128]{2,1,0:T(8,128)(2,1)} %param.12) | copy-start | bytes 1572868
  8.6 40.7 %all-to-all-start.1 = ((bf16[128,16,128]{2,0,1:T(8,128)(2,1)}), bf16[128,16,128]{2,0,1:T(8,128)(2,1)S(1)}, u32[]{:S(2)}, u32[]{:S(2)}) async-start(bf16[128,16,128]{2,0,1:T(8,128)(2,1)} %copy.119), calls=%async_computation.1 | async-start | bytes 1048576 | tf_op jit(solution)/shard_map/all_to_all | solution.py:53
  49.3 14.2 %all-to-all-start.2 = ((bf16[128,16,128]{2,0,1:T(8,128)(2,1)}), bf16[128,16,128]{2,0,1:T(8,128)(2,1)S(1)}, u32[]{:S(2)}, u32[]{:S(2)}) async-start(bf16[128,16,128]{2,0,1:T(8,128)(2,1)} %copy.125), calls=%async_computation.2 | async-start | bytes 1048576 | tf_op jit(solution)/shard_map/all_to_all | solution.py:54
  63.5 22.5 %all-to-all-start = ((bf16[128,16,128]{2,0,1:T(8,128)(2,1)}), bf16[128,16,128]{2,0,1:T(8,128)(2,1)S(1)}, u32[]{:S(2)}, u32[]{:S(2)}) async-start(bf16[128,16,128]{2,0,1:T(8,128)(2,1)} %copy.117), calls=%async_computation | async-start | bytes 1048576 | tf_op jit(solution)/shard_map/all_to_all | solution.py:52
  67.8 159.2 %all-gather.3.cloned.1.call-start = ((), (), s32[]{:S(2)}) async-start(), calls=%async_computation.4 | async-start | bytes 4259840 | tf_op jit(solution)/shard_map/all_gather | solution.py:117
  70.4 40.1 %collective-permute-start.1 = (bf16[2,4,64,2,128]{4,2,3,1,0:T(8,128)(2,1)S(1)}, bf16[2,4,64,2,128]{4,2,3,1,0:T(8,128)(2,1)S(1)}, u32[]{:S(2)}, u32[]{:S(2)}) collective-permute-start(bf16[2,4,64,2,128]{4,2,3,1,0:T(8,128)(2,1)S(1)} %pad_maximum_fusion), channel_id=1, source_target_pairs={{1,0},{2,1},{3,2},{4,3},{5,4},{6,5},{7,6},{8,7},{9,8},{10,9},{11,1... | collective-permute-start | bytes 786440 | tf_op jit(solution)/shard_map/ppermute | solution.py:12
  71.7 38.8 %collective-permute-start = (bf16[2,4,64,2,128]{4,2,3,1,0:T(8,128)(2,1)S(1)}, bf16[2,4,64,2,128]{4,2,3,1,0:T(8,128)(2,1)S(1)}, u32[]{:S(2)}, u32[]{:S(2)}) collective-permute-start(bf16[2,4,64,2,128]{4,2,3,1,0:T(8,128)(2,1)S(1)} %pad_maximum_fusion), channel_id=1, source_target_pairs={{0,1},{1,2},{2,3},{3,4},{4,5},{5,6},{6,7},{7,8},{8,9},{9,10},{10,1... | collective-permute-start | bytes 786440 | tf_op jit(solution)/shard_map/ppermute | solution.py:12
  75.8 18.2 %collective-permute-start.2 = (bf16[2,2,64,2,128]{4,2,3,1,0:T(8,128)(2,1)S(1)}, bf16[2,2,64,2,128]{4,2,3,1,0:T(8,128)(2,1)}, u32[]{:S(2)}, u32[]{:S(2)}) collective-permute-start(bf16[2,2,64,2,128]{4,2,3,1,0:T(8,128)(2,1)S(1)} %pad_maximum_fusion.1), channel_id=1, source_target_pairs={{0,2},{1,3},{2,4},{3,5},{4,6},{5,7},{6,8},{7,9},{8,10},{9,11},{10,... | collective-permute-start | bytes 393224 | tf_op jit(solution)/shard_map/ppermute | solution.py:12
  77.7 18.7 %collective-permute-start.5 = (bf16[2,2,64,2,128]{4,2,3,1,0:T(8,128)(2,1)S(1)}, bf16[2,2,64,2,128]{4,2,3,1,0:T(8,128)(2,1)}, u32[]{:S(2)}, u32[]{:S(2)}) collective-permute-start(bf16[2,2,64,2,128]{4,2,3,1,0:T(8,128)(2,1)S(1)} %pad_maximum_fusion.1), channel_id=1, source_target_pairs={{3,0},{4,1},{5,2},{6,3},{7,4},{8,5},{9,6},{10,7},{11,8},{12,9},{13... | collective-permute-start | bytes 393224 | tf_op jit(solution)/shard_map/ppermute | solution.py:12
  79.0 18.3 %collective-permute-start.4 = (bf16[2,2,64,2,128]{4,2,3,1,0:T(8,128)(2,1)S(1)}, bf16[2,2,64,2,128]{4,2,3,1,0:T(8,128)(2,1)S(1)}, u32[]{:S(2)}, u32[]{:S(2)}) collective-permute-start(bf16[2,2,64,2,128]{4,2,3,1,0:T(8,128)(2,1)S(1)} %pad_maximum_fusion.1), channel_id=1, source_target_pairs={{0,3},{1,4},{2,5},{3,6},{4,7},{5,8},{6,9},{7,10},{8,11},{9,12},{10... | collective-permute-start | bytes 393224 | tf_op jit(solution)/shard_map/ppermute | solution.py:12
  92.9 12.5 %copy-start.11 = (pred[16,128]{1,0:T(8,128)(4,1)S(1)}, pred[16,128]{1,0:T(8,128)(4,1)}, u32[]{:S(2)}) copy-start(pred[16,128]{1,0:T(8,128)(4,1)} %broadcast_in_dim.280) | copy-start | bytes 6148
  94.0 12.1 %copy-start.9 = (pred[16,128]{1,0:T(8,128)(4,1)S(1)}, pred[16,128]{1,0:T(8,128)(4,1)}, u32[]{:S(2)}) copy-start(pred[16,128]{1,0:T(8,128)(4,1)} %broadcast_in_dim.277) | copy-start | bytes 6148
  94.0 11.1 %collective-permute-start.3 = (bf16[2,2,64,2,128]{4,2,3,1,0:T(8,128)(2,1)S(1)}, bf16[2,2,64,2,128]{4,2,3,1,0:T(8,128)(2,1)S(1)}, u32[]{:S(2)}, u32[]{:S(2)}) collective-permute-start(bf16[2,2,64,2,128]{4,2,3,1,0:T(8,128)(2,1)S(1)} %pad_maximum_fusion.1), channel_id=1, source_target_pairs={{2,0},{3,1},{4,2},{5,3},{6,4},{7,5},{8,6},{9,7},{10,8},{11,9},{12,... | collective-permute-start | bytes 393224 | tf_op jit(solution)/shard_map/ppermute | solution.py:12
  96.4 10.3 %copy-start.10 = (pred[16,128]{1,0:T(8,128)(4,1)S(1)}, pred[16,128]{1,0:T(8,128)(4,1)}, u32[]{:S(2)}) copy-start(pred[16,128]{1,0:T(8,128)(4,1)} %broadcast_in_dim.274) | copy-start | bytes 6148
  106.1 3.3 copy-start.8
  120.7 106.3 %copy-start.1 = (s32[64]{0:T(128)S(1)}, s32[64]{0:T(128)}, u32[]{:S(2)}) copy-start(s32[64]{0:T(128)} %param.17) | copy-start | bytes 772
  120.7 106.3 %copy-start.2 = (s32[64]{0:T(128)S(1)}, s32[64]{0:T(128)}, u32[]{:S(2)}) copy-start(s32[64]{0:T(128)} %param.16) | copy-start | bytes 772
  255.5 1.3 copy-start.3
  318.1 1.3 copy-start.3
  380.6 1.3 copy-start.3
  396.3 1.3 copy-start.3
  458.9 1.3 copy-start.3
  474.5 1.3 copy-start.3
  (28 other events, 31.8 us)
Sparse Core Ops, SparseCore 0:
  86.9 140.0 all-gather.2
where the time goes:
time: 513 us; the launch traced here: 511 us
  local copies, waits for them, and re-layouts  137 us (27%)
  waiting for transfers between devices  114 us (22%)
  other arithmetic  89 us (17%)
  matrix products  68.6 us (13%)
  starting transfers between devices  36.4 us (7%)
  between operations  31 us (6%)
  blocking collectives  23.4 us (5%)
  loops' own time  12.5 us (2%)
    all_gather x1, waiting for transfers between devices, local(): gathered = lax.all_gather(anchor_pair, 'frame', axis=0, tiled=True)  103 us
    reduce_sum x23, other arithmetic, group_terms(): group_totals = jnp.sum(weights, axis=4)  45.4 us
    convert_element_type x16, local copies, waits for them, and re-layouts, group_terms(): weights.astype(jnp.bfloat16)  42.6 us
    while x16, matrix products  36.3 us
    all_to_all x1, blocking collectives, local(): lax.all_to_all(output, 'head', split_axis=0, concat_axis=1, tiled=True)  23.4 us
    reduce_sum x16, other arithmetic, absorb(): jnp.sum(factors[..., None] * group_sums, axis=3)  21 us
    dot_general x18, matrix products, group_terms(): jnp.einsum('qahd,gnhd->hqagn', query_blocks, key_rows, preferred_element_...  19 us
    ppermute x6, starting transfers between devices, passed_along(): return lax.ppermute(block, axis, route)  16.9 us
  transfers between devices with their start and end apart: 10, of which 3 were waited for; matrix products, arithmetic and copies ran while one was open for 10% of the time, Pallas kernels for 0%

commit v1 on v0

--- a/solution.py
+++ b/solution.py
@@ -2,6 +2,7 @@
 import jax.numpy as jnp
 from jax import lax
 from jax.sharding import PartitionSpec as P
+from jax.lax import all_to_all, axis_size
 
 masked_score = -1e30
 
@@ -114,7 +115,12 @@
             )
     anchor_block = (frame_blocks - offsets[frame_index] % frame_blocks) % frame_blocks
     anchor_pair = jnp.stack([key_blocks[anchor_block], value_blocks[anchor_block]])[None]
-    gathered = lax.all_gather(anchor_pair, "frame", axis=0, tiled=True)
+    gathered = jnp.concatenate(
+        all_to_all(
+            jnp.stack([anchor_pair for _ in range(axis_size("frame"))], axis=0), "frame", 0, 0
+        ),
+        axis=0,
+    )
     piece_frames = gathered.shape[0]
     group_width = 4
     grouped = gathered.reshape(

time: 513 us -> 553 us (1.078)
  waiting for transfers between devices: 114 us -> 154 us
  starting transfers between devices: 36.4 us -> 59.1 us
  between operations: 31 us -> 17.6 us
  blocking collectives: 23.4 us -> 16.6 us
    ppermute x6, waiting for transfers between devices: 7.73 us -> 131 us  [passed_along(): return lax.ppermute(block, axis, route)]
    all_gather x1 -> x0, waiting for transfers between devices: 103 us -> none  [local(): gathered = lax.all_gather(anchor_pair, 'frame', axis=0, tiled=True)]
    all_to_all x0 -> x1, starting transfers between devices: none -> 14.4 us  [local(): all_to_all(jnp.stack([anchor_pair for _ in range(axis_size('frame'))], ax...]
    ppermute x6, starting transfers between devices: 16.9 us -> 25.8 us  [passed_along(): return lax.ppermute(block, axis, route)]
    all_to_all x1, waiting for transfers between devices: 0.01 us -> 7.41 us  [local(): lax.all_to_all(keys, 'head', split_axis=1, concat_axis=0, tiled=True)]
    all_to_all x1, blocking collectives: 23.4 us -> 16.6 us  [local(): lax.all_to_all(output, 'head', split_axis=0, concat_axis=1, tiled=True)]
    all_to_all x1, waiting for transfers between devices: 0.01 us -> 6.65 us  [local(): lax.all_to_all(queries, 'head', split_axis=1, concat_axis=0, tiled=True)]
    all_to_all x1, waiting for transfers between devices: 2.51 us -> 8.45 us  [local(): lax.all_to_all(values, 'head', split_axis=1, concat_axis=0, tiled=True)]
  transfers between devices with their start and end apart: 10 -> 10, of which waited for: 3 -> 4; matrix products, arithmetic and copies ran while one was open for 10% -> 8% of each run, Pallas kernels for 0% -> 0%
where the time goes in v1:
time: 553 us; the launch traced here: 549 us
  waiting for transfers between devices  154 us (28%)
  local copies, waits for them, and re-layouts  134 us (24%)
  other arithmetic  88.3 us (16%)
  matrix products  67.5 us (12%)
  starting transfers between devices  59.1 us (11%)
  between operations  17.6 us (3%)
  blocking collectives  16.6 us (3%)
  loops' own time  12.5 us (2%)
    ppermute x6, waiting for transfers between devices, passed_along(): return lax.ppermute(block, axis, route)  131 us
    reduce_sum x23, other arithmetic, group_terms(): group_totals = jnp.sum(weights, axis=4)  45 us
    convert_element_type x16, local copies, waits for them, and re-layouts, group_terms(): weights.astype(jnp.bfloat16)  42.6 us
    while x16, matrix products  36.3 us
    ppermute x6, starting transfers between devices, passed_along(): return lax.ppermute(block, axis, route)  25.8 us
    reduce_sum x16, other arithmetic, absorb(): jnp.sum(factors[..., None] * group_sums, axis=3)  21.3 us
    dot_general x18, matrix products, group_terms(): jnp.einsum('qahd,gnhd->hqagn', query_blocks, key_rows, preferred_element_...  17.9 us
    while x80, local copies, waits for them, and re-layouts  17.1 us
  transfers between devices with their start and end apart: 10, of which 4 were waited for; matrix products, arithmetic and copies ran while one was open for 8% of the time, Pallas kernels for 0%

profile of v1, /device:TPU:1, one launch (start us, length us, event | category | flops | bytes accessed | tf_op | source)
XLA Modules:
  0.0 549.1 jit_solution(17221768444950155614)
XLA Ops:
  2.0 10.2 %all-to-all-start.1 = ((bf16[128,16,128]{2,0,1:T(8,128)(2,1)}), bf16[128,16,128]{2,0,1:T(8,128)(2,1)S(1)}, u32[]{:S(2)}, u32[]{:S(2)}) async-start(bf16[128,16,128]{2,0,1:T(8,128)(2,1)} %copy.120), calls=%async_computation.1 | async-start | bytes 1048576 | tf_op jit(solution)/shard_map/all_to_all | solution.py:54
  14.2 7.4 %all-to-all-done.1 = bf16[128,16,128]{2,0,1:T(8,128)(2,1)S(1)} async-done(((bf16[128,16,128]{2,0,1:T(8,128)(2,1)}), bf16[128,16,128]{2,0,1:T(8,128)(2,1)S(1)}, u32[]{:S(2)}, u32[]{:S(2)}) %all-to-all-start.1) | async-done | bytes 524320 | tf_op jit(solution)/shard_map/all_to_all | solution.py:54
  21.7 4.4 all-to-all-start.2
  27.0 8.4 %all-to-all-done.2 = bf16[128,16,128]{2,0,1:T(8,128)(2,1)S(1)} async-done(((bf16[128,16,128]{2,0,1:T(8,128)(2,1)}), bf16[128,16,128]{2,0,1:T(8,128)(2,1)S(1)}, u32[]{:S(2)}, u32[]{:S(2)}) %all-to-all-start.2) | async-done | bytes 524320 | tf_op jit(solution)/shard_map/all_to_all | solution.py:55
  35.4 4.4 all-to-all-start
  42.5 6.7 %all-to-all-done = bf16[128,16,128]{2,0,1:T(8,128)(2,1)S(1)} async-done(((bf16[128,16,128]{2,0,1:T(8,128)(2,1)}), bf16[128,16,128]{2,0,1:T(8,128)(2,1)S(1)}, u32[]{:S(2)}, u32[]{:S(2)}) %all-to-all-start) | async-done | bytes 524320 | tf_op jit(solution)/shard_map/all_to_all | solution.py:53
  49.1 3.0 stack.34
  52.2 14.4 %all-to-all-start.3 = ((bf16[64,1,2,64,2,128]{5,3,4,2,1,0:T(8,128)(2,1)}), bf16[64,1,2,64,2,128]{5,3,4,2,1,0:T(8,128)(2,1)}, u32[]{:S(2)}, u32[]{:S(2)}) async-start(bf16[64,1,2,64,2,128]{5,3,4,2,1,0:T(8,128)(2,1)} %stack.34), calls=%async_computation.3 | async-start | bytes 8388608 | tf_op jit(solution)/shard_map/all_to_all | solution.py:119
  96.8 5.8 %collective-permute-start.4 = (bf16[2,2,64,2,128]{4,2,3,1,0:T(8,128)(2,1)S(1)}, bf16[2,2,64,2,128]{4,2,3,1,0:T(8,128)(2,1)S(1)}, u32[]{:S(2)}, u32[]{:S(2)}) collective-permute-start(bf16[2,2,64,2,128]{4,2,3,1,0:T(8,128)(2,1)S(1)} %pad_maximum_fusion.1), channel_id=1, source_target_pairs={{0,3},{1,4},{2,5},{3,6},{4,7},{5,8},{6,9},{7,10},{8,11},{9,12},{10... | collective-permute-start | bytes 393224 | tf_op jit(solution)/shard_map/ppermute | solution.py:13
  103.9 5.6 %collective-permute-start.2 = (bf16[2,2,64,2,128]{4,2,3,1,0:T(8,128)(2,1)S(1)}, bf16[2,2,64,2,128]{4,2,3,1,0:T(8,128)(2,1)S(1)}, u32[]{:S(2)}, u32[]{:S(2)}) collective-permute-start(bf16[2,2,64,2,128]{4,2,3,1,0:T(8,128)(2,1)S(1)} %pad_maximum_fusion.1), channel_id=1, source_target_pairs={{0,2},{1,3},{2,4},{3,5},{4,6},{5,7},{6,8},{7,9},{8,10},{9,11},{10,... | collective-permute-start | bytes 393224 | tf_op jit(solution)/shard_map/ppermute | solution.py:13
  117.4 131.3 %collective-permute-done.5 = bf16[2,2,64,2,128]{4,2,3,1,0:T(8,128)(2,1)S(1)} collective-permute-done((bf16[2,2,64,2,128]{4,2,3,1,0:T(8,128)(2,1)S(1)}, bf16[2,2,64,2,128]{4,2,3,1,0:T(8,128)(2,1)S(1)}, u32[]{:S(2)}, u32[]{:S(2)}) %collective-permute-start.5) | collective-permute-done | bytes 131104 | tf_op jit(solution)/shard_map/ppermute | solution.py:13
  248.7 10.5 %collective-permute-start = (bf16[2,4,64,2,128]{4,2,3,1,0:T(8,128)(2,1)S(1)}, bf16[2,4,64,2,128]{4,2,3,1,0:T(8,128)(2,1)S(1)}, u32[]{:S(2)}, u32[]{:S(2)}) collective-permute-start(bf16[2,4,64,2,128]{4,2,3,1,0:T(8,128)(2,1)S(1)} %pad_maximum_fusion), channel_id=1, source_target_pairs={{0,1},{1,2},{2,3},{3,4},{4,5},{5,6},{6,7},{7,8},{8,9},{9,10},{10,1... | collective-permute-start | bytes 786440 | tf_op jit(solution)/shard_map/ppermute | solution.py:13
  274.9 3.0 fusion.58
  277.9 251.2 %while.16 = (s32[]{:T(128)}, f32[2,16,64]{2,1,0:T(8,128)S(1)}, f32[2,16,64]{2,1,0:T(8,128)S(1)}, f32[2,16,64,128]{3,2,1,0:T(8,128)}, s32[]{:T(128)}, /*index=5*/...) while((s32[]{:T(128)}, f32[2,16,64]{2,1,0:T(8,128)S(1)}, ...), condition=%wide.region_22.25_spmd, body=%wide.region_16.24_spmd.sunk | while | flops 276053440 | bytes 31036728 | solution.py:146
  285.8 2.7 copy.174
  301.5 2.7 copy.174
  332.8 2.7 copy.174
  379.9 2.7 copy.174
  411.3 2.7 copy.174
  427.0 2.7 copy.174
  442.7 2.7 copy.174
  458.4 2.7 copy.174
  489.8 2.7 copy.174
  531.2 16.6 %all_to_all.68 = bf16[1024,2,128]{2,1,0:T(2,128)(2,1)S(1)} all-to-all(bf16[1024,2,128]{2,1,0:T(2,128)(2,1)S(1)} %bitcast.475), channel_id=1, replica_groups=mesh['head'=8,'frame'=64] {'head'}, dimensions={0} | all-to-all | bytes 1048576 | tf_op jit(solution)/shard_map/all_to_all | solution.py:151
  (577 shorter events, 263.4 us)
Async XLA Ops:
  0.0 82.1 %copy-start = (s32[64,16,16]{0,2,1:T(8,128)S(1)}, s32[64,16,16]{0,2,1:T(8,128)}, u32[]{:S(2)}) copy-start(s32[64,16,16]{0,2,1:T(8,128)} %param.15) | copy-start | bytes 196612
  0.0 26.0 %copy-start.5 = (bf16[128,16,128]{2,1,0:T(8,128)(2,1)S(1)}, bf16[128,16,128]{2,1,0:T(8,128)(2,1)}, u32[]{:S(2)}) copy-start(bf16[128,16,128]{2,1,0:T(8,128)(2,1)} %param.12) | copy-start | bytes 1572868
  0.0 39.8 %copy-start.1 = (s32[64]{0:T(128)S(1)}, s32[64]{0:T(128)}, u32[]{:S(2)}) copy-start(s32[64]{0:T(128)} %param.17) | copy-start | bytes 772
  2.0 19.6 %all-to-all-start.1 = ((bf16[128,16,128]{2,0,1:T(8,128)(2,1)}), bf16[128,16,128]{2,0,1:T(8,128)(2,1)S(1)}, u32[]{:S(2)}, u32[]{:S(2)}) async-start(bf16[128,16,128]{2,0,1:T(8,128)(2,1)} %copy.120), calls=%async_computation.1 | async-start | bytes 1048576 | tf_op jit(solution)/shard_map/all_to_all | solution.py:54
  21.7 13.7 %all-to-all-start.2 = ((bf16[128,16,128]{2,0,1:T(8,128)(2,1)}), bf16[128,16,128]{2,0,1:T(8,128)(2,1)S(1)}, u32[]{:S(2)}, u32[]{:S(2)}) async-start(bf16[128,16,128]{2,0,1:T(8,128)(2,1)} %copy.126), calls=%async_computation.2 | async-start | bytes 1048576 | tf_op jit(solution)/shard_map/all_to_all | solution.py:55
  35.4 13.7 %all-to-all-start = ((bf16[128,16,128]{2,0,1:T(8,128)(2,1)}), bf16[128,16,128]{2,0,1:T(8,128)(2,1)S(1)}, u32[]{:S(2)}, u32[]{:S(2)}) async-start(bf16[128,16,128]{2,0,1:T(8,128)(2,1)} %copy.118), calls=%async_computation | async-start | bytes 1048576 | tf_op jit(solution)/shard_map/all_to_all | solution.py:53
  52.2 25.5 %copy-start.2 = (s32[64]{0:T(128)S(1)}, s32[64]{0:T(128)}, u32[]{:S(2)}) copy-start(s32[64]{0:T(128)} %param.16) | copy-start | bytes 772
  52.2 225.7 %all-to-all-start.3 = ((bf16[64,1,2,64,2,128]{5,3,4,2,1,0:T(8,128)(2,1)}), bf16[64,1,2,64,2,128]{5,3,4,2,1,0:T(8,128)(2,1)}, u32[]{:S(2)}, u32[]{:S(2)}) async-start(bf16[64,1,2,64,2,128]{5,3,4,2,1,0:T(8,128)(2,1)} %stack.34), calls=%async_computation.3 | async-start | bytes 8388608 | tf_op jit(solution)/shard_map/all_to_all | solution.py:119
  95.5 153.2 %collective-permute-start.5 = (bf16[2,2,64,2,128]{4,2,3,1,0:T(8,128)(2,1)S(1)}, bf16[2,2,64,2,128]{4,2,3,1,0:T(8,128)(2,1)S(1)}, u32[]{:S(2)}, u32[]{:S(2)}) collective-permute-start(bf16[2,2,64,2,128]{4,2,3,1,0:T(8,128)(2,1)S(1)} %pad_maximum_fusion.1), channel_id=1, source_target_pairs={{3,0},{4,1},{5,2},{6,3},{7,4},{8,5},{9,6},{10,7},{11,8},{12,9},{13... | collective-permute-start | bytes 393224 | tf_op jit(solution)/shard_map/ppermute | solution.py:13
  96.8 162.5 %collective-permute-start.4 = (bf16[2,2,64,2,128]{4,2,3,1,0:T(8,128)(2,1)S(1)}, bf16[2,2,64,2,128]{4,2,3,1,0:T(8,128)(2,1)S(1)}, u32[]{:S(2)}, u32[]{:S(2)}) collective-permute-start(bf16[2,2,64,2,128]{4,2,3,1,0:T(8,128)(2,1)S(1)} %pad_maximum_fusion.1), channel_id=1, source_target_pairs={{0,3},{1,4},{2,5},{3,6},{4,7},{5,8},{6,9},{7,10},{8,11},{9,12},{10... | collective-permute-start | bytes 393224 | tf_op jit(solution)/shard_map/ppermute | solution.py:13
  102.6 156.7 %collective-permute-start.3 = (bf16[2,2,64,2,128]{4,2,3,1,0:T(8,128)(2,1)S(1)}, bf16[2,2,64,2,128]{4,2,3,1,0:T(8,128)(2,1)S(1)}, u32[]{:S(2)}, u32[]{:S(2)}) collective-permute-start(bf16[2,2,64,2,128]{4,2,3,1,0:T(8,128)(2,1)S(1)} %pad_maximum_fusion.1), channel_id=1, source_target_pairs={{2,0},{3,1},{4,2},{5,3},{6,4},{7,5},{8,6},{9,7},{10,8},{11,9},{12,... | collective-permute-start | bytes 393224 | tf_op jit(solution)/shard_map/ppermute | solution.py:13
  103.9 155.4 %collective-permute-start.2 = (bf16[2,2,64,2,128]{4,2,3,1,0:T(8,128)(2,1)S(1)}, bf16[2,2,64,2,128]{4,2,3,1,0:T(8,128)(2,1)S(1)}, u32[]{:S(2)}, u32[]{:S(2)}) collective-permute-start(bf16[2,2,64,2,128]{4,2,3,1,0:T(8,128)(2,1)S(1)} %pad_maximum_fusion.1), channel_id=1, source_target_pairs={{0,2},{1,3},{2,4},{3,5},{4,6},{5,7},{6,8},{7,9},{8,10},{9,11},{10,... | collective-permute-start | bytes 393224 | tf_op jit(solution)/shard_map/ppermute | solution.py:13
  116.1 148.5 %collective-permute-start.1 = (bf16[2,4,64,2,128]{4,2,3,1,0:T(8,128)(2,1)S(1)}, bf16[2,4,64,2,128]{4,2,3,1,0:T(8,128)(2,1)S(1)}, u32[]{:S(2)}, u32[]{:S(2)}) collective-permute-start(bf16[2,4,64,2,128]{4,2,3,1,0:T(8,128)(2,1)S(1)} %pad_maximum_fusion), channel_id=1, source_target_pairs={{1,0},{2,1},{3,2},{4,3},{5,4},{6,5},{7,6},{8,7},{9,8},{10,9},{11,1... | collective-permute-start | bytes 786440 | tf_op jit(solution)/shard_map/ppermute | solution.py:13
  248.7 16.1 %collective-permute-start = (bf16[2,4,64,2,128]{4,2,3,1,0:T(8,128)(2,1)S(1)}, bf16[2,4,64,2,128]{4,2,3,1,0:T(8,128)(2,1)S(1)}, u32[]{:S(2)}, u32[]{:S(2)}) collective-permute-start(bf16[2,4,64,2,128]{4,2,3,1,0:T(8,128)(2,1)S(1)} %pad_maximum_fusion), channel_id=1, source_target_pairs={{0,1},{1,2},{2,3},{3,4},{4,5},{5,6},{6,7},{7,8},{8,9},{9,10},{10,1... | collective-permute-start | bytes 786440 | tf_op jit(solution)/shard_map/ppermute | solution.py:13
  290.7 1.3 copy-start.3
  306.4 1.3 copy-start.3
  322.1 1.3 copy-start.3
  337.8 1.3 copy-start.3
  353.5 1.3 copy-start.3
  369.2 1.3 copy-start.3
  384.9 1.3 copy-start.3
  400.6 1.3 copy-start.3
  416.3 1.3 copy-start.3
  432.0 1.3 copy-start.3
  (22 other events, 25.2 us)
